TPU v7x, 32 devices: a whole 2x2x4 slice. The times are simulated.
32 devices in a mesh: groups: 2 (over y), mp: 4 (over x, core), hidden: 4 (over z).
Axes of the slice: x: 2, y: 2, z: 4, core: 2. Of those that a mesh axis runs over, the one named last changes fastest.
Arguments:
- inputs: bfloat16 [2048, 8192], P(('groups', 'hidden'), 'mp'), parts along dimension 0, as said below
- out_grad: bfloat16 [2048, 16384], P(('groups', 'mp'), 'hidden'), parts along dimension 0, as said below
- weight: float32 [8192, 16384], P('mp', 'hidden'), may hold values from -0.0625 to 0.0625
- noise: bfloat16 [2, 16384, 16384], P(None, ('groups', 'mp'), 'hidden'), parts along dimension 1, may hold values from -6 to 6
Outputs:
- outputs: bfloat16 [2048, 16384], P(('groups', 'mp'), 'hidden'), parts along dimension 0
- in_grad: bfloat16 [2048, 8192], P(('groups', 'hidden'), 'mp'), parts along dimension 0
- update: float32 [8192, 32768], P('mp', ('groups', 'hidden')), parts along dimension 1
There are 2 independent parts, one for each index of `groups`. A program takes and returns all parts, laid end to end along the dimension named above; an argument that names none is the same for every part. Nothing has to cross between parts.
Inputs may be any that keep to these rules, and one draw needn't show every extreme that they name: `inputs`: Real-valued activations whose rows and columns carry independent scales. `out_grad`: Real-valued gradients whose rows and columns carry independent scales; examples differ in overall size.
All inputs are finite; a program needn't handle non-finite values.
Results may differ from a plain program's by a relative error of at most 0.0049.
Values may be sent and summed in bfloat16 or wider, within the bound.
A program may use at most 256 MiB of HBM per device.

v0:
```python
import math

import jax
import jax.numpy as jnp
from jax import lax
from jax.sharding import PartitionSpec as P

D = 8192
FF = 16384
SEQ = 64
EXAMPLES = 16


def shards(inputs, out_grad, weight, noise):
    weight_half = weight.astype(jnp.bfloat16)
    feature_rows = lax.all_gather(inputs, "hidden", axis=0, tiled=True)
    unit_rows = lax.all_gather(out_grad, "mp", axis=0, tiled=True)
    picked = feature_rows
    outputs = lax.psum_scatter(
        jnp.dot(picked, weight_half, preferred_element_type=jnp.float32),
        "mp",
        scatter_dimension=0,
        tiled=True,
    ).astype(jnp.bfloat16)
    picked = unit_rows
    in_grad = lax.psum_scatter(
        lax.dot_general(
            picked, weight_half, (((1,), (1,)), ((), ())), preferred_element_type=jnp.float32
        ),
        "hidden",
        scatter_dimension=0,
        tiled=True,
    ).astype(jnp.bfloat16)
    feature_blocks = feature_rows.reshape(EXAMPLES, SEQ, feature_rows.shape[1])
    unit_blocks = unit_rows.reshape(EXAMPLES, SEQ, unit_rows.shape[1])
    feature_gram = jnp.einsum(
        "bsd,btd->bst", feature_blocks, feature_blocks, preferred_element_type=jnp.float32
    )
    unit_gram = jnp.einsum(
        "bsd,btd->bst", unit_blocks, unit_blocks, preferred_element_type=jnp.float32
    )
    feature_gram = lax.psum(feature_gram.astype(jnp.bfloat16), "mp").astype(jnp.float32)
    unit_gram = lax.psum(unit_gram.astype(jnp.bfloat16), "hidden").astype(jnp.float32)
    squares = jnp.sum(feature_gram * unit_gram, axis=(1, 2))
    clip_norm = math.sqrt(SEQ * D * FF)
    factor = jnp.minimum(1.0, clip_norm / jnp.sqrt(squares + 1e-06))
    token_factor = jnp.repeat(factor, SEQ)[:, None]
    scaled_grad = (unit_rows.astype(jnp.float32) * token_factor).astype(jnp.bfloat16)
    weight_grad = lax.dot_general(
        feature_rows, scaled_grad, (((0,), (0,)), ((), ())), preferred_element_type=jnp.float32
    )
    band_noise = noise[0].astype(jnp.float32) - 0.6 * noise[1].astype(jnp.float32)
    update = (weight_grad * (math.sqrt(D * FF) / clip_norm) + 4.0 * band_noise) / EXAMPLES
    return (outputs, in_grad, update)


def solution(mesh):
    in_specs = (
        P(("groups", "hidden"), "mp"),
        P(("groups", "mp"), "hidden"),
        P("mp", "hidden"),
        P(None, ("groups", "mp"), "hidden"),
    )
    out_specs = (
        P(("groups", "mp"), "hidden"),
        P(("groups", "hidden"), "mp"),
        P("mp", ("groups", "hidden")),
    )
    return jax.shard_map(shards, mesh=mesh, in_specs=in_specs, out_specs=out_specs, check_vma=False)
```

profile of v0, /device:TPU:0, one launch (start us, length us, event | category | flops | bytes accessed | tf_op | source)
XLA Modules:
  0.0 510.3 jit_solution(1098056114129314794)
XLA Ops:
  7.2 0.7 all-gather.3.cloned.1.call-update
  7.9 0.7 all-gather.5.cloned.1.call-update
  8.6 0.0 all-reduce.3.cloned.1.call-start
  8.7 84.3 %all-gather.3.cloned.1.call-done = bf16[1024,2048]{1,0:T(8,128)(2,1)} async-done(((bf16[256,2048]{1,0:T(8,128)(2,1)}), bf16[1024,2048]{1,0:T(8,128)(2,1)}) %all-gather.3.cloned.1.call-update) | async-done | bytes 4194320 | tf_op jit(solution)/shard_map/all_gather | solution.py:16
  93.0 5.4 %convolution_convert_fusion.1 = bf16[16,64,64]{2,1,0:T(8,128)(2,1)} fusion(bf16[16,64,2048]{2,1,0:T(8,128)(2,1)} %bitcast.16), kind=kOutput, calls=%fused_computation.9 | convolution fusion | flops 268500992 | bytes 4325376 | tf_op jit(solution)/shard_map/bsd,btd->bst/dot_general | solution.py:36
  98.5 0.0 all-reduce.5.cloned.1.call-start
  98.5 52.9 %all-gather.5.cloned.1.call-done = bf16[1024,4096]{1,0:T(8,128)(2,1)} async-done(((bf16[256,4096]{1,0:T(8,128)(2,1)}), bf16[1024,4096]{1,0:T(8,128)(2,1)}) %all-gather.5.cloned.1.call-update) | async-done | bytes 8388624 | tf_op jit(solution)/shard_map/all_gather | solution.py:17
  151.4 8.8 %convolution_convert_fusion = bf16[16,64,64]{2,1,0:T(8,128)(2,1)} fusion(bf16[16,64,4096]{2,1,0:T(8,128)(2,1)} %bitcast.15), kind=kOutput, calls=%fused_computation.8 | convolution fusion | flops 536936448 | bytes 8519680 | tf_op jit(solution)/shard_map/bsd,btd->bst/dot_general | solution.py:39
  160.2 0.0 reduce-scatter.5.cloned.1.call-start
  160.2 25.3 %fusion.2 = f32[1024,2048]{1,0:T(8,128)} fusion(bf16[1024,4096]{1,0:T(8,128)(2,1)} %all-gather.5.cloned.1.call-done, f32[2048,4096]{1,0:T(8,128)} %param.6), kind=kOutput, calls=%fused_computation.4 | convolution fusion | flops 17188257792 | bytes 50331648 | tf_op jit(solution)/shard_map/dot_general | solution.py:27
  185.6 0.0 reduce-scatter.3.cloned.1.call-start
  185.7 25.1 %fusion.4 = f32[1024,4096]{1,0:T(8,128)} fusion(bf16[1024,2048]{1,0:T(8,128)(2,1)} %all-gather.3.cloned.1.call-done, f32[2048,4096]{1,0:T(8,128)} %param.6), kind=kOutput, calls=%fused_computation.6 | convolution fusion | flops 17188257792 | bytes 54525952 | tf_op jit(solution)/shard_map/dot_general | solution.py:20
  210.8 23.5 %fusion.6 = (bf16[1,2048,4096]{2,1,0:T(8,128)(2,1)}, bf16[1,2048,4096]{2,1,0:T(8,128)(2,1)}) fusion(bf16[2,2048,4096]{2,1,0:T(8,128)(2,1)} %param.7), kind=kLoop, calls=%fused_computation.12 | loop fusion | bytes 67108864 | tf_op jit(solution)/shard_map/slice | solution.py:52
  234.2 22.6 %copy.10 = bf16[1,2048,4096]{1,2,0:T(8,128)(2,1)} copy(bf16[1,2048,4096]{2,1,0:T(8,128)(2,1)} %get-tuple-element.6) | data formatting | bytes 33554432
  256.8 22.5 %copy.11 = bf16[1,2048,4096]{1,2,0:T(8,128)(2,1)} copy(bf16[1,2048,4096]{2,1,0:T(8,128)(2,1)} %get-tuple-element.7) | data formatting | bytes 33554432
  279.3 1.2 multiply_reduce_fusion
  280.5 0.1 broadcast_in_dim.3
  280.6 0.1 mul.39
  280.7 35.8 %fusion = f32[2048,4096]{0,1:T(8,128)} fusion(bf16[1,2048,4096]{1,2,0:T(8,128)(2,1)} %copy.11, bf16[1,2048,4096]{1,2,0:T(8,128)(2,1)} %copy.10, bf16[1024,2048]{1,0:T(8,128)(2,1)} %all-gather.3.cloned.1.call-done, bf16[1024,4096]{1,0:T(8,128)(2,1)} %all-gather.5.cloned.1.call-done, f32[1024]{0:T(1024)S(1)} %mul.39), kind=kOutput, calls=%fused_computation.1 | convolution fusion | flops 17259560960 | bytes 79695872 | tf_op jit(solution)/shard_map/dot_general | solution.py:49
  316.5 31.1 %copy.9 = f32[2048,4096]{1,0:T(8,128)} copy(f32[2048,4096]{0,1:T(8,128)} %fusion) | data formatting | bytes 67108864
  347.6 23.9 %reduce-scatter.5.cloned.1.call-done = f32[256,2048]{1,0:T(8,128)} async-done(((f32[1024,2048]{1,0:T(8,128)}), f32[256,2048]{1,0:T(8,128)}) %reduce-scatter.5.cloned.1.call-update) | async-done | bytes 2097168 | tf_op jit(solution)/shard_map/reduce_scatter | solution.py:26
  371.5 2.7 convert_element_type.37
  374.3 125.4 %reduce-scatter.3.cloned.1.call-done = f32[256,4096]{1,0:T(8,128)} async-done(((f32[1024,4096]{1,0:T(8,128)}), f32[256,4096]{1,0:T(8,128)}) %reduce-scatter.3.cloned.1.call-update) | async-done | bytes 4194320 | tf_op jit(solution)/shard_map/reduce_scatter | solution.py:19
  499.7 3.8 convert_element_type.36
  (9 shorter events, 0.2 us)
Async XLA Ops:
  7.2 85.9 %all-gather.3.cloned.1.call-start = ((), (), s32[]{:S(2)}) async-start(), calls=%async_computation.2 | async-start | bytes 5242880 | tf_op jit(solution)/shard_map/all_gather | solution.py:16
  7.9 143.5 %all-gather.5.cloned.1.call-start = ((), (), s32[]{:S(2)}) async-start(), calls=%async_computation.4 | async-start | bytes 10485760 | tf_op jit(solution)/shard_map/all_gather | solution.py:17
  8.6 270.6 %all-reduce.3.cloned.1.call-start = ((), (), s32[]{:S(2)}) async-start(), calls=%async_computation.6 | async-start | bytes 524288 | tf_op jit(solution)/shard_map/psum | solution.py:42
  98.5 180.8 %all-reduce.5.cloned.1.call-start = ((), (), s32[]{:S(2)}) async-start(), calls=%async_computation.7 | async-start | bytes 524288 | tf_op jit(solution)/shard_map/psum | solution.py:43
  160.2 211.4 %reduce-scatter.5.cloned.1.call-start = ((), (), s32[]{:S(2)}) async-start(), calls=%async_computation.5 | async-start | bytes 10485760 | tf_op jit(solution)/shard_map/reduce_scatter | solution.py:26
  185.6 314.1 %reduce-scatter.3.cloned.1.call-start = ((), (), s32[]{:S(2)}) async-start(), calls=%async_computation.3 | async-start | bytes 20971520 | tf_op jit(solution)/shard_map/reduce_scatter | solution.py:19
Sparse Core Ops, SparseCore 0:
  9.5 83.4 all-gather.2
  94.6 56.7 all-gather.4
  154.3 32.2 all-reduce.2
  189.4 35.3 all-reduce.4
  227.0 144.4 reduce-scatter.4
  374.0 125.6 reduce-scatter.2
where the time goes:
time: 512 us; the launch traced here: 510 us
  waiting for transfers between devices  288 us (56%)
  matrix products  100 us (20%)
  local copies, waits for them, and re-layouts  99.7 us (19%)
  between operations  14.1 us (3%)
  other arithmetic  7.75 us (2%)
    reduce_scatter x1, waiting for transfers between devices, shards(): lax.psum_scatter(jnp.dot(picked, weight_half, preferred_element_type=jnp....  125 us
    all_gather x1, waiting for transfers between devices, shards(): feature_rows = lax.all_gather(inputs, 'hidden', axis=0, tiled=True)  84.3 us
    unnamed x3, local copies, waits for them, and re-layouts  76.2 us
    all_gather x1, waiting for transfers between devices, shards(): unit_rows = lax.all_gather(out_grad, 'mp', axis=0, tiled=True)  52.9 us
    dot_general x1, matrix products, shards(): lax.dot_general(feature_rows, scaled_grad, (((0,), (0,)), ((), ())), pref...  35.8 us
    dot_general x1, matrix products, shards(): lax.dot_general(picked, weight_half, (((1,), (1,)), ((), ())), preferred_...  25.3 us
    dot_general x1, matrix products, shards(): jnp.dot(picked, weight_half, preferred_element_type=jnp.float32)  25.1 us
    reduce_scatter x1, waiting for transfers between devices, shards(): lax.psum_scatter(lax.dot_general(picked, weight_half, (((1,), (1,)), ((),...  23.9 us
  transfers between devices with their start and end apart: 6, of which 4 were waited for; matrix products, arithmetic and copies ran while one was open for 40% of the time, Pallas kernels for 0%

commit v1 on v0

v1 whole, which is shorter than its diff:
```python
import math

import jax
import jax.numpy as jnp
from jax import lax
from jax.experimental import pallas as pl
from jax.experimental.pallas import tpu as pltpu
from jax.sharding import PartitionSpec as P


D = 8192
FF = 16384
SEQ = 64
EXAMPLES = 16
PARTS = 4


def ring_up(value, axis, n):
    return lax.ppermute(value, axis, [(i, (i + 1) % n) for i in range(n)])


def swap(value, axis, n, bit):
    return lax.ppermute(value, axis, [(i, i ^ bit) for i in range(n)])


def bits(n):
    return [1 << i for i in range(n.bit_length() - 1)]


def after(value, event):
    return lax.optimization_barrier((value, event))[0]


def put(buffer, block, index):
    return lax.dynamic_update_slice(buffer, block, (index * block.shape[0], 0))


def take(buffer, index, rows):
    return lax.dynamic_slice_in_dim(buffer, index * rows, rows, axis=0)


def update_kernel(gain, features_ref, grad_ref, noise_ref, *rest):
    out_ref = rest[-1]
    weight_grad = jnp.dot(
        features_ref[...], grad_ref[...], preferred_element_type=jnp.float32
    )
    band = noise_ref[0].astype(jnp.float32) - 0.6 * noise_ref[1].astype(jnp.float32)
    out_ref[...] = (weight_grad * gain + 4.0 * band) * (1.0 / EXAMPLES)


def update_part(features_t, scaled_grad, noise, gain, part, parts, so_far):
    m, tokens = features_t.shape
    n = scaled_grad.shape[1]
    tm, tn = min(m, 512), min(n // parts, 1024)
    steps = n // parts // tn
    at = part * steps
    in_specs = [
        pl.BlockSpec((tm, tokens), lambda j, i: (i, 0)),
        pl.BlockSpec((tokens, tn), lambda j, i: (0, at + j)),
        pl.BlockSpec((2, tm, tn), lambda j, i: (0, i, at + j)),
    ]
    operands = [features_t, scaled_grad, noise]
    aliases = {}
    if so_far is not None:
        in_specs.append(pl.BlockSpec(memory_space=pl.ANY))
        operands.append(so_far)
        aliases = {3: 0}
    return pl.pallas_call(
        lambda *refs: update_kernel(gain, *refs),
        grid=(steps, m // tm),
        in_specs=in_specs,
        out_specs=pl.BlockSpec((tm, tn), lambda j, i: (i, at + j)),
        out_shape=jax.ShapeDtypeStruct((m, n), jnp.float32),
        input_output_aliases=aliases,
        cost_estimate=pl.CostEstimate(
            flops=2 * m * n * tokens // parts,
            bytes_accessed=12 * m * n // parts,
            transcendentals=0,
        ),
        compiler_params=pltpu.CompilerParams(vmem_limit_bytes=40 * 1024 * 1024),
    )(*operands)


def block_gram(rows):
    blocks = rows.reshape(-1, SEQ, rows.shape[1])
    return jnp.einsum("bsd,btd->bst", blocks, blocks, preferred_element_type=jnp.float32)


def shards(n_mp, n_hidden, inputs, out_grad, weight, noise):
    mp, hidden = lax.axis_index("mp"), lax.axis_index("hidden")
    in_rows, width = inputs.shape
    out_rows, units = out_grad.shape
    tokens = in_rows * n_hidden

    have = {0: out_grad}
    bit = n_mp // 2
    while bit:
        have.update({o ^ bit: swap(v, "mp", n_mp, bit) for o, v in have.items()})
        bit //= 2

    weight_half = lax.optimization_barrier(weight.astype(jnp.bfloat16))

    feature_rows = jnp.zeros((tokens, width), jnp.bfloat16)
    partial = jnp.zeros((tokens, units), jnp.bfloat16)
    block = inputs
    events = []
    for step in range(n_hidden):
        at = lax.rem(hidden - step + n_hidden, n_hidden)
        later = None
        if step < n_hidden - 1:
            later = ring_up(block, "hidden", n_hidden)
        product = jnp.dot(block, weight_half, preferred_element_type=jnp.float32)
        partial = put(partial, product.astype(jnp.bfloat16), at)
        feature_rows = put(feature_rows, block, at)
        block = later
        if later is not None:
            events.append(later)

    def event(index):
        return events[min(index, len(events) - 1)][:8, :128]

    unit_rows = jnp.zeros((tokens, units), jnp.bfloat16)
    for offset, value in have.items():
        unit_rows = put(unit_rows, value, mp ^ offset)

    own = in_rows % SEQ == 0 and in_rows == out_rows
    if own:
        feature_gram, unit_gram = block_gram(inputs), block_gram(out_grad)
        for k, bit in enumerate(bits(n_mp)):
            arrived = after(swap(feature_gram, "mp", n_mp, bit), event(k))
            feature_gram = feature_gram + arrived
        for k, bit in enumerate(bits(n_hidden)):
            arrived = after(swap(unit_gram, "hidden", n_hidden, bit), event(k))
            unit_gram = unit_gram + arrived
        mine = jnp.sum(feature_gram * unit_gram, axis=(1, 2))
        mine = jnp.where(mp == hidden, mine, 0.0)
        squares = lax.dynamic_update_slice(
            jnp.zeros((tokens // SEQ,), jnp.float32), mine, (hidden * (in_rows // SEQ),)
        )
        for bit in bits(n_mp):
            squares = squares + after(swap(squares, "mp", n_mp, bit), event(2))

    first = partial.reshape(-1, 2, out_rows, units)
    mine = lax.rem(mp, 2)
    keep = lax.dynamic_index_in_dim(first, mine, 1, keepdims=False)
    send = lax.dynamic_index_in_dim(first, 1 - mine, 1, keepdims=False)
    near = swap(send, "mp", n_mp, 1)

    pieces = 2
    columns = width // pieces
    shares = []
    operand = unit_rows
    for piece in range(pieces):
        share = lax.dot_general(
            operand,
            weight_half[piece * columns : (piece + 1) * columns],
            (((1,), (1,)), ((), ())),
            preferred_element_type=jnp.float32,
        )
        shares.append(lax.optimization_barrier(share))
        if piece == 0:
            near = after(near, shares[0][:8, :128])
            left = (keep.astype(jnp.float32) + near.astype(jnp.float32)).astype(jnp.bfloat16)
            operand = after(unit_rows, left[0, :8, :128])
    bit = 2
    while bit < n_mp:
        pairs = left.reshape(-1, 2, out_rows, units)
        mine = lax.rem(mp // bit, 2)
        keep = lax.dynamic_index_in_dim(pairs, mine, 1, keepdims=False)
        send = lax.dynamic_index_in_dim(pairs, 1 - mine, 1, keepdims=False)
        arrived = swap(send, "mp", n_mp, bit)
        left = (keep.astype(jnp.float32) + arrived.astype(jnp.float32)).astype(jnp.bfloat16)
        bit *= 2
    outputs = left.reshape(out_rows, units)

    done = []
    for piece in range(pieces):
        running = None
        for step in range(n_hidden):
            at = lax.rem(hidden - 1 - step + 2 * n_hidden, n_hidden)
            term = take(shares[piece], at, in_rows)
            if step:
                arrived = ring_up(running, "hidden", n_hidden)
                term = term + arrived.astype(jnp.float32)
            running = term.astype(jnp.bfloat16)
        done.append(running)
    in_grad = jnp.concatenate(done, axis=1)

    if own:
        for bit in bits(n_hidden):
            arrived = after(swap(squares, "hidden", n_hidden, bit), shares[0][:8, :128])
            squares = squares + arrived
    if not own:
        feature_gram = lax.psum(block_gram(feature_rows).astype(jnp.bfloat16), "mp").astype(jnp.float32)
        unit_gram = lax.psum(block_gram(unit_rows).astype(jnp.bfloat16), "hidden").astype(jnp.float32)
        squares = jnp.sum(feature_gram * unit_gram, axis=(1, 2))
    clip_norm = math.sqrt(SEQ * D * FF)
    factor = jnp.minimum(1.0, clip_norm / jnp.sqrt(squares + 1e-06))
    token_factor = jnp.repeat(factor, SEQ)[:, None]
    scaled_grad = (unit_rows.astype(jnp.float32) * token_factor).astype(jnp.bfloat16)
    features_t = feature_rows.T
    gain = math.sqrt(D * FF) / clip_norm
    parts = PARTS if units % (PARTS * 1024) == 0 else 1
    update = None
    for part in range(parts):
        update = update_part(features_t, scaled_grad, noise, gain, part, parts, update)
    return (outputs, in_grad, update)


def solution(mesh):
    n_mp, n_hidden = mesh.shape["mp"], mesh.shape["hidden"]
    in_specs = (
        P(("groups", "hidden"), "mp"),
        P(("groups", "mp"), "hidden"),
        P("mp", "hidden"),
        P(None, ("groups", "mp"), "hidden"),
    )
    out_specs = (
        P(("groups", "mp"), "hidden"),
        P(("groups", "hidden"), "mp"),
        P("mp", ("groups", "hidden")),
    )

    def body(*args):
        return shards(n_mp, n_hidden, *args)

    return jax.shard_map(body, mesh=mesh, in_specs=in_specs, out_specs=out_specs, check_vma=False)
```

time: 512 us -> 257 us (0.50)
  waiting for transfers between devices: 288 us -> 42.1 us
  local copies, waits for them, and re-layouts: 99.7 us -> 40.3 us
  Pallas kernels: 0 us -> 43.6 us
  other arithmetic: 7.75 us -> 44.3 us
  matrix products: 100 us -> 63.5 us
  starting transfers between devices: 0.24 us -> 21.4 us
  between operations: 14.1 us -> 0.85 us
    reduce_scatter x2 -> x0, waiting for transfers between devices: 149 us -> none  [the longest x1 125 us: shards(): lax.psum_scatter(jnp.dot(picked, weight_half, preferred_element_type=jnp....]
    all_gather x2 -> x0, waiting for transfers between devices: 137 us -> none  [the longest x1 84.3 us: shards(): feature_rows = lax.all_gather(inputs, 'hidden', axis=0, tiled=True)]
    unnamed x3 -> x19, local copies, waits for them, and re-layouts: 76.2 us -> 5.67 us
    pallas_call x0 -> x4, Pallas kernels: none -> 43.6 us  [update_part(): pl.pallas_call(lambda *refs: update_kernel(gain, *refs), grid=(steps, m /...]
    ppermute x0 -> x22, waiting for transfers between devices: none -> 42.1 us  [the longest x9 36.4 us: ring_up(): return lax.ppermute(value, axis, [(i, (i + 1) % n) for i in range(n)])]
    dot_general x5 -> x8, matrix products: 100 us -> 63.5 us  [the longest x4 34.7 us: shards(): product = jnp.dot(block, weight_half, preferred_element_type=jnp.float32)]
    convert_element_type x2 -> x9, other arithmetic: 6.5 us -> 39.7 us  [the longest x1 17.4 us: shards(): weight_half = lax.optimization_barrier(weight.astype(jnp.bfloat16))]
    slice x1 -> x0, local copies, waits for them, and re-layouts: 23.5 us -> none  [shards(): noise[0].astype(jnp.float32) - 0.6 * noise[1].astype(jnp.float32)]
  transfers between devices with their start and end apart: 6 -> 22, of which waited for: 4 -> 7; matrix products, arithmetic and copies ran while one was open for 40% -> 56% of each run, Pallas kernels for 0% -> 17%
where the time goes in v1:
time: 257 us; the launch traced here: 256 us
  matrix products  63.5 us (25%)
  other arithmetic  44.3 us (17%)
  Pallas kernels  43.6 us (17%)
  waiting for transfers between devices  42.1 us (16%)
  local copies, waits for them, and re-layouts  40.3 us (16%)
  starting transfers between devices  21.4 us (8%)
    pallas_call x4, Pallas kernels, update_part(): pl.pallas_call(lambda *refs: update_kernel(gain, *refs), grid=(steps, m /...  43.6 us
    ppermute x9, waiting for transfers between devices, ring_up(): return lax.ppermute(value, axis, [(i, (i + 1) % n) for i in range(n)])  36.4 us
    dot_general x4, matrix products, shards(): product = jnp.dot(block, weight_half, preferred_element_type=jnp.float32)  34.7 us
    dot_general x2, matrix products, shards(): lax.dot_general(operand, weight_half[piece * columns:(piece + 1) * column...  23.9 us
    convert_element_type x1, other arithmetic, shards(): weight_half = lax.optimization_barrier(weight.astype(jnp.bfloat16))  17.4 us
    dynamic_update_slice x8, local copies, waits for them, and re-layouts, put(): return lax.dynamic_update_slice(buffer, block, (index * block.shape[0], 0))  15.1 us
    ppermute x13, starting transfers between devices, swap(): return lax.ppermute(value, axis, [(i, i ^ bit) for i in range(n)])  11.5 us
    convert_element_type x1, other arithmetic, shards(): (unit_rows.astype(jnp.float32) * token_factor).astype(jnp.bfloat16)  10.1 us
  transfers between devices with their start and end apart: 22, of which 7 were waited for; matrix products, arithmetic and copies ran while one was open for 56% of the time, Pallas kernels for 17%

profile of v1, /device:TPU:0, one launch (start us, length us, event | category | flops | bytes accessed | tf_op | source)
XLA Modules:
  0.0 256.0 jit_solution(113303959887541352)
XLA Ops:
  13.6 17.4 %convert_element_type.86 = bf16[2048,4096]{1,0:T(8,128)(2,1)} convert(f32[2048,4096]{1,0:T(8,128)} %param.6) | non-fusion elementwise | flops 8388608 | bytes 50331648 | tf_op jit(solution)/shard_map/convert_element_type | solution.py:101
  30.9 4.3 %broadcast.25.clone = bf16[1024,4096]{1,0:T(8,128)(2,1)} broadcast(bf16[]{:T(256)} %constant.79.clone.1), dimensions={} | broadcast | bytes 8388610 | tf_op jit(solution)/shard_map/broadcast.9
  35.2 11.4 %fusion.8 = bf16[1024,4096]{1,0:T(8,128)(2,1)} fusion(bf16[1024,4096]{1,0:T(8,128)(2,1)} %broadcast.25.clone, s32[]{:T(128)S(6)} %select_n.72, bf16[256,2048]{1,0:T(8,128)(2,1)S(1)} %copy-done.2, bf16[2048,4096]{1,0:T(8,128)(2,1)} %convert_element_type.86), kind=kOutput, calls=%fused_computation.14 | convolution fusion | flops 4296015872 | bytes 19922948 | tf_op jit(solution)/shard_map/dot_general | solution.py:112
  46.7 4.3 %broadcast.25.clone.1 = bf16[1024,4096]{1,0:T(8,128)(2,1)} broadcast(bf16[]{:T(256)} %constant.79.clone.1), dimensions={} | broadcast | bytes 8388610 | tf_op jit(solution)/shard_map/broadcast.9
  58.5 3.1 %collective-permute-start.17 = (f32[4,64,64]{2,1,0:T(8,128)S(1)}, f32[4,64,64]{2,1,0:T(8,128)S(1)}, u32[]{:S(2)}, u32[]{:S(2)}) collective-permute-start(f32[4,64,64]{2,1,0:T(8,128)S(1)} %add.198), channel_id=1, source_target_pairs={{0,2},{1,3},{2,0},{3,1},{4,6},{5,7},{6,4},{7,5},{8,10},{9,11},{10,... | collective-permute-start | bytes 196616 | tf_op jit(solution)/shard_map/ppermute | solution.py:23
  63.0 11.8 %fusion.7 = bf16[1024,4096]{1,0:T(8,128)(2,1)} fusion(bf16[1024,4096]{1,0:T(8,128)(2,1)} %fusion.8, s32[]{:T(128)S(6)} %select_n.73, bf16[256,2048]{0,1:T(8,128)(2,1)S(1)} %collective-permute-done, bf16[2048,4096]{1,0:T(8,128)(2,1)} %convert_element_type.86), kind=kOutput, calls=%fused_computation.12 | convolution fusion | flops 4296015872 | bytes 19922948 | tf_op jit(solution)/shard_map/dot_general | solution.py:112
  75.8 13.3 %collective-permute-done.1 = bf16[256,2048]{0,1:T(8,128)(2,1)S(1)} collective-permute-done((bf16[256,2048]{0,1:T(8,128)(2,1)S(1)}, bf16[256,2048]{0,1:T(8,128)(2,1)S(1)}, u32[]{:S(2)}, u32[]{:S(2)}) %collective-permute-start.1) | collective-permute-done | bytes 1048608 | tf_op jit(solution)/shard_map/ppermute | solution.py:19
  91.9 3.3 %constant_dynamic-update-slice_fusion.6 = bf16[1024,4096]{1,0:T(8,128)(2,1)} fusion(bf16[1024,4096]{1,0:T(8,128)(2,1)} %constant_dynamic-update-slice_fusion.7, bf16[256,4096]{1,0:T(8,128)(2,1)} %collective-permute-done.4, s32[]{:T(128)S(6)} %select_n.79), kind=kLoop, calls=%fused_computation.35 | loop fusion | bytes 4194308 | tf_op jit(solution)/shard_map/dynamic_update_slice | solution.py:35
  95.2 3.2 %constant_dynamic-update-slice_fusion.5 = bf16[1024,4096]{1,0:T(8,128)(2,1)} fusion(bf16[1024,4096]{1,0:T(8,128)(2,1)} %constant_dynamic-update-slice_fusion.6, bf16[256,4096]{1,0:T(8,128)(2,1)} %collective-permute-done.5, s32[]{:T(128)S(6)} %select_n.80), kind=kLoop, calls=%fused_computation.34 | loop fusion | bytes 4194308 | tf_op jit(solution)/shard_map/dynamic_update_slice | solution.py:35
  98.4 5.7 %fusion.6 = bf16[1024,4096]{1,0:T(8,128)(2,1)} fusion(bf16[1024,4096]{1,0:T(8,128)(2,1)} %fusion.7, s32[]{:T(128)S(6)} %select_n.74, bf16[256,2048]{0,1:T(8,128)(2,1)S(1)} %collective-permute-done.1, bf16[2048,4096]{1,0:T(8,128)(2,1)S(1)} %bitcast.28), kind=kOutput, calls=%fused_computation.10 | convolution fusion | flops 4296015872 | bytes 19922948 | tf_op jit(solution)/shard_map/dot_general | solution.py:112
  104.1 13.2 %collective-permute-done.2 = bf16[256,2048]{0,1:T(8,128)(2,1)S(1)} collective-permute-done((bf16[256,2048]{0,1:T(8,128)(2,1)S(1)}, bf16[256,2048]{0,1:T(8,128)(2,1)S(1)}, u32[]{:S(2)}, u32[]{:S(2)}) %collective-permute-start.2) | collective-permute-done | bytes 1048608 | tf_op jit(solution)/shard_map/ppermute | solution.py:19
  119.5 5.8 %fusion.5 = bf16[1024,4096]{1,0:T(8,128)(2,1)} fusion(bf16[1024,4096]{1,0:T(8,128)(2,1)} %fusion.6, s32[]{:T(128)S(6)} %select_n.75, bf16[256,2048]{0,1:T(8,128)(2,1)S(1)} %collective-permute-done.2, bf16[2048,4096]{1,0:T(8,128)(2,1)S(1)} %bitcast.28), kind=kOutput, calls=%fused_computation.8 | convolution fusion | flops 4296015872 | bytes 19922948 | tf_op jit(solution)/shard_map/dot_general | solution.py:112
  125.2 4.7 %dynamic-slice_bitcast_fusion = bf16[2,256,4096]{2,1,0:T(8,128)(2,1)} fusion(bf16[2,2,256,4096]{3,2,1,0:T(8,128)(2,1)} %bitcast, s32[]{:T(128)S(6)} %select_n.77), kind=kLoop, calls=%fused_computation.16 | loop fusion | bytes 8388612 | tf_op jit(solution)/shard_map/jit(dynamic_index_in_dim)/squeeze | solution.py:146
  132.5 12.6 %fusion.2 = f32[1024,1024]{1,0:T(8,128)} fusion(bf16[1024,4096]{1,0:T(8,128)(2,1)} %constant_dynamic-update-slice_fusion.4, bf16[2048,4096]{1,0:T(8,128)(2,1)S(1)} %bitcast.28), kind=kOutput, calls=%fused_computation.3 | convolution fusion | flops 8589934592 | bytes 20971520 | tf_op jit(solution)/shard_map/dot_general | solution.py:154
  145.1 11.2 %fusion = f32[1024,1024]{1,0:T(8,128)S(1)} fusion(bf16[1024,4096]{1,0:T(8,128)(2,1)} %constant_dynamic-update-slice_fusion.4, bf16[2048,4096]{1,0:T(8,128)(2,1)S(1)} %bitcast.28), kind=kOutput, calls=%fused_computation.1 | convolution fusion | flops 8589934592 | bytes 20971520 | tf_op jit(solution)/shard_map/dot_general | solution.py:154
  161.8 10.1 %multiply_convert_fusion.refs_1_ = bf16[1024,4096]{1,0:T(8,128)(2,1)} fusion(bf16[1024,4096]{1,0:T(8,128)(2,1)} %constant_dynamic-update-slice_fusion.4, f32[1024]{0:T(1024)S(1)} %mul.71), kind=kLoop, calls=%fused_computation | loop fusion | flops 12582912 | bytes 16781312 | tf_op jit(solution)/shard_map/convert_element_type | solution.py:200
  172.0 3.4 %copy-done = bf16[1024,4096]{1,0:T(8,128)(2,1)S(1)} copy-done((bf16[1024,4096]{1,0:T(8,128)(2,1)S(1)}, bf16[1024,4096]{1,0:T(8,128)(2,1)}, u32[]{:S(2)}) %copy-start) | copy-done | bytes 8388632
  175.4 10.9 %shard_map.67.refs_3_ = f32[2048,4096]{1,0:T(8,128)} custom-call(bf16[2048,1024]{1,0:T(8,128)(2,1)} %bitcast.4.refs_0_, bf16[1024,4096]{1,0:T(8,128)(2,1)S(1)} %copy-done, bf16[2,2048,4096]{2,1,0:T(8,128)(2,1)} %refs_2_.7), custom_call_target="tpu_custom_call" | custom-call | flops 4294967296 | bytes 25165824 | tf_op jit(solution)/shard_map/pallas_call | solution.py:68
  186.2 10.9 %shard_map.68.refs_3_ = f32[2048,4096]{1,0:T(8,128)} custom-call(bf16[2048,1024]{1,0:T(8,128)(2,1)} %bitcast.4.refs_0_, bf16[1024,4096]{1,0:T(8,128)(2,1)S(1)} %copy-done, bf16[2,2048,4096]{2,1,0:T(8,128)(2,1)} %refs_2_.7, f32[2048,4096]{1,0:T(8,128)} %shard_map.67.refs_3_), custom_call_target="tpu_custom_call", output_to_operand_aliasing={{}: (3, {})} | custom-call | flops 4294967296 | bytes 25165824 | tf_op jit(solution)/shard_map/pallas_call | solution.py:68
  200.6 5.0 %fusion.4 = bf16[2,256,4096]{2,1,0:T(8,128)(2,1)S(1)} fusion(bf16[2,256,4096]{2,1,0:T(8,128)(2,1)} %collective-permute-done.3, bf16[2,2,256,4096]{3,2,1,0:T(8,128)(2,1)} %bitcast, s32[]{:T(128)S(6)} %select_n.76), kind=kLoop, calls=%fused_computation.6 | loop fusion | flops 8388608 | bytes 12582916 | tf_op jit(solution)/shard_map/convert_element_type | solution.py:163
  209.5 10.9 %shard_map.69.refs_3_ = f32[2048,4096]{1,0:T(8,128)} custom-call(bf16[2048,1024]{1,0:T(8,128)(2,1)} %bitcast.4.refs_0_, bf16[1024,4096]{1,0:T(8,128)(2,1)S(1)} %copy-done, bf16[2,2048,4096]{2,1,0:T(8,128)(2,1)} %refs_2_.7, f32[2048,4096]{1,0:T(8,128)} %shard_map.68.refs_3_), custom_call_target="tpu_custom_call", output_to_operand_aliasing={{}: (3, {})} | custom-call | flops 4294967296 | bytes 25165824 | tf_op jit(solution)/shard_map/pallas_call | solution.py:68
  227.4 10.9 %shard_map.70 = f32[2048,4096]{1,0:T(8,128)} custom-call(bf16[2048,1024]{1,0:T(8,128)(2,1)} %bitcast.4.refs_0_, bf16[1024,4096]{1,0:T(8,128)(2,1)S(1)} %copy-done, bf16[2,2048,4096]{2,1,0:T(8,128)(2,1)} %refs_2_.7, f32[2048,4096]{1,0:T(8,128)} %shard_map.69.refs_3_), custom_call_target="tpu_custom_call", output_to_operand_aliasing={{}: (3, {})} | custom-call | flops 4294967296 | bytes 25165824 | tf_op jit(solution)/shard_map/pallas_call | solution.py:68
  239.8 7.8 %collective-permute-done.13 = bf16[256,1024]{1,0:T(8,128)(2,1)S(1)} collective-permute-done((bf16[256,1024]{1,0:T(8,128)(2,1)}, bf16[256,1024]{1,0:T(8,128)(2,1)S(1)}, u32[]{:S(2)}, u32[]{:S(2)}) %collective-permute-start.13) | collective-permute-done | bytes 524320 | tf_op jit(solution)/shard_map/ppermute | solution.py:19
  248.8 5.1 %collective-permute-done.7 = bf16[1,256,4096]{2,1,0:T(8,128)(2,1)S(1)} collective-permute-done((bf16[1,256,4096]{2,1,0:T(8,128)(2,1)}, bf16[1,256,4096]{2,1,0:T(8,128)(2,1)S(1)}, u32[]{:S(2)}, u32[]{:S(2)}) %collective-permute-start.7) | collective-permute-done | bytes 2097184 | tf_op jit(solution)/shard_map/ppermute | solution.py:23
  (89 shorter events, 55.0 us)
Async XLA Ops:
  0.6 90.0 %collective-permute-start.4 = (bf16[256,4096]{1,0:T(8,128)(2,1)}, bf16[256,4096]{1,0:T(8,128)(2,1)}, u32[]{:S(2)}, u32[]{:S(2)}) collective-permute-start(bf16[256,4096]{1,0:T(8,128)(2,1)} %param.5), channel_id=1, source_target_pairs={{0,8},{4,12},{8,0},{12,4},{1,9},{5,13},{9,1},{13,5},{2,10},{6,14},... | collective-permute-start | bytes 6291464 | tf_op jit(solution)/shard_map/ppermute | solution.py:23
  3.7 91.5 %collective-permute-start.5 = (bf16[256,4096]{1,0:T(8,128)(2,1)}, bf16[256,4096]{1,0:T(8,128)(2,1)}, u32[]{:S(2)}, u32[]{:S(2)}) collective-permute-start(bf16[256,4096]{1,0:T(8,128)(2,1)} %param.5), channel_id=1, source_target_pairs={{0,4},{4,0},{8,12},{12,8},{1,5},{5,1},{9,13},{13,9},{2,6},{6,2},{1... | collective-permute-start | bytes 6291464 | tf_op jit(solution)/shard_map/ppermute | solution.py:23
  5.7 52.6 %collective-permute-start.14 = (f32[4,64,64]{2,1,0:T(8,128)S(1)}, f32[4,64,64]{2,1,0:T(8,128)S(1)}, u32[]{:S(2)}, u32[]{:S(2)}) collective-permute-start(f32[4,64,64]{2,1,0:T(8,128)S(1)} %fusion.11), channel_id=1, source_target_pairs={{0,4},{4,0},{8,12},{12,8},{1,5},{5,1},{9,13},{13,9},{2,6},{6,2},{1... | collective-permute-start | bytes 196616 | tf_op jit(solution)/shard_map/ppermute | solution.py:23
  9.2 48.2 %collective-permute-start.16 = (f32[4,64,64]{2,1,0:T(8,128)S(1)}, f32[4,64,64]{2,1,0:T(8,128)}, u32[]{:S(2)}, u32[]{:S(2)}) collective-permute-start(f32[4,64,64]{2,1,0:T(8,128)S(1)} %fusion.12), channel_id=1, source_target_pairs={{0,1},{1,0},{2,3},{3,2},{4,5},{5,4},{6,7},{7,6},{8,9},{9,8},{10,11... | collective-permute-start | bytes 196616 | tf_op jit(solution)/shard_map/ppermute | solution.py:23
  13.1 44.3 %collective-permute-start = (bf16[256,2048]{0,1:T(8,128)(2,1)}, bf16[256,2048]{0,1:T(8,128)(2,1)S(1)}, u32[]{:S(2)}, u32[]{:S(2)}) collective-permute-start(bf16[256,2048]{0,1:T(8,128)(2,1)} %copy.10), channel_id=1, source_target_pairs={{0,1},{1,2},{2,3},{3,0},{4,5},{5,6},{6,7},{7,4},{8,9},{9,10},{10,1... | collective-permute-start | bytes 3145736 | tf_op jit(solution)/shard_map/ppermute | solution.py:19
  58.4 31.4 %collective-permute-start.15 = (f32[4,64,64]{2,1,0:T(8,128)S(1)}, f32[4,64,64]{2,1,0:T(8,128)S(1)}, u32[]{:S(2)}, u32[]{:S(2)}) collective-permute-start(f32[4,64,64]{2,1,0:T(8,128)S(1)} %add.196), channel_id=1, source_target_pairs={{0,8},{4,12},{8,0},{12,4},{1,9},{5,13},{9,1},{13,5},{2,10},{6,14},... | collective-permute-start | bytes 196616 | tf_op jit(solution)/shard_map/ppermute | solution.py:23
  58.5 31.3 %collective-permute-start.17 = (f32[4,64,64]{2,1,0:T(8,128)S(1)}, f32[4,64,64]{2,1,0:T(8,128)S(1)}, u32[]{:S(2)}, u32[]{:S(2)}) collective-permute-start(f32[4,64,64]{2,1,0:T(8,128)S(1)} %add.198), channel_id=1, source_target_pairs={{0,2},{1,3},{2,0},{3,1},{4,6},{5,7},{6,4},{7,5},{8,10},{9,11},{10,... | collective-permute-start | bytes 196616 | tf_op jit(solution)/shard_map/ppermute | solution.py:23
  61.5 27.6 %collective-permute-start.1 = (bf16[256,2048]{0,1:T(8,128)(2,1)S(1)}, bf16[256,2048]{0,1:T(8,128)(2,1)S(1)}, u32[]{:S(2)}, u32[]{:S(2)}) collective-permute-start(bf16[256,2048]{0,1:T(8,128)(2,1)S(1)} %collective-permute-done), channel_id=1, source_target_pairs={{0,1},{1,2},{2,3},{3,0},{4,5},{5,6},{6,7},{7,4},{8,9},{9,10},{10,1... | collective-permute-start | bytes 3145736 | tf_op jit(solution)/shard_map/ppermute | solution.py:19
  63.0 35.4 %slice-start.1 = ((s8[16777216]{0:T(1024)(128)(4,1)}), s8[4194304]{0:T(1024)(128)(4,1)S(1)}, s32[]{:S(2)}) async-start(s8[16777216]{0:T(1024)(128)(4,1)} %bitcast.27), calls=%async_computation.1 | async-start | bytes 8388608
  63.0 35.4 %slice-start.2 = ((s8[16777216]{0:T(1024)(128)(4,1)}), s8[4194304]{0:T(1024)(128)(4,1)S(1)}, s32[]{:S(2)}) async-start(s8[16777216]{0:T(1024)(128)(4,1)} %bitcast.27), calls=%async_computation.2 | async-start | bytes 8388608
  90.0 27.4 %collective-permute-start.18 = (f32[16]{0:T(128)S(1)}, f32[16]{0:T(128)S(1)}, u32[]{:S(2)}, u32[]{:S(2)}) collective-permute-start(f32[16]{0:T(128)S(1)} %fusion.10), channel_id=1, source_target_pairs={{0,4},{4,0},{8,12},{12,8},{1,5},{5,1},{9,13},{13,9},{2,6},{6,2},{1... | collective-permute-start | bytes 200 | tf_op jit(solution)/shard_map/ppermute | solution.py:23
  90.0 27.4 %collective-permute-start.2 = (bf16[256,2048]{0,1:T(8,128)(2,1)S(1)}, bf16[256,2048]{0,1:T(8,128)(2,1)S(1)}, u32[]{:S(2)}, u32[]{:S(2)}) collective-permute-start(bf16[256,2048]{0,1:T(8,128)(2,1)S(1)} %collective-permute-done.1), channel_id=1, source_target_pairs={{0,1},{1,2},{2,3},{3,0},{4,5},{5,6},{6,7},{7,4},{8,9},{9,10},{10,1... | collective-permute-start | bytes 3145736 | tf_op jit(solution)/shard_map/ppermute | solution.py:19
  90.7 40.4 %collective-permute-start.6 = (bf16[256,4096]{1,0:T(8,128)(2,1)}, bf16[256,4096]{1,0:T(8,128)(2,1)S(1)}, u32[]{:S(2)}, u32[]{:S(2)}) collective-permute-start(bf16[256,4096]{1,0:T(8,128)(2,1)} %collective-permute-done.4), channel_id=1, source_target_pairs={{0,4},{4,0},{8,12},{12,8},{1,5},{5,1},{9,13},{13,9},{2,6},{6,2},{1... | collective-permute-start | bytes 6291464 | tf_op jit(solution)/shard_map/ppermute | solution.py:23
  117.6 13.5 %collective-permute-start.19 = (f32[16]{0:T(128)S(1)}, f32[16]{0:T(128)S(1)}, u32[]{:S(2)}, u32[]{:S(2)}) collective-permute-start(f32[16]{0:T(128)S(1)} %add_dynamic-update-slice_fusion), channel_id=1, source_target_pairs={{0,8},{4,12},{8,0},{12,4},{1,9},{5,13},{9,1},{13,5},{2,10},{6,14},... | collective-permute-start | bytes 200 | tf_op jit(solution)/shard_map/ppermute | solution.py:23
  129.9 70.7 %collective-permute-start.3 = (bf16[2,256,4096]{2,1,0:T(8,128)(2,1)}, bf16[2,256,4096]{2,1,0:T(8,128)(2,1)}, u32[]{:S(2)}, u32[]{:S(2)}) collective-permute-start(bf16[2,256,4096]{2,1,0:T(8,128)(2,1)} %dynamic-slice_bitcast_fusion), channel_id=1, source_target_pairs={{0,4},{4,0},{8,12},{12,8},{1,5},{5,1},{9,13},{13,9},{2,6},{6,2},{1... | collective-permute-start | bytes 12582920 | tf_op jit(solution)/shard_map/ppermute | solution.py:23
  131.1 25.4 %collective-permute-start.20 = (f32[16]{0:T(128)S(1)}, f32[16]{0:T(128)S(1)}, u32[]{:S(2)}, u32[]{:S(2)}) collective-permute-start(f32[16]{0:T(128)S(1)} %add.202), channel_id=1, source_target_pairs={{0,1},{1,0},{2,3},{3,2},{4,5},{5,4},{6,7},{7,6},{8,9},{9,8},{10,11... | collective-permute-start | bytes 200 | tf_op jit(solution)/shard_map/ppermute | solution.py:23
  156.4 5.3 %collective-permute-start.21 = (f32[16]{0:T(128)S(1)}, f32[16]{0:T(128)S(1)}, u32[]{:S(2)}, u32[]{:S(2)}) collective-permute-start(f32[16]{0:T(128)S(1)} %add.203), channel_id=1, source_target_pairs={{0,2},{1,3},{2,0},{3,1},{4,6},{5,7},{6,4},{7,5},{8,10},{9,11},{10,... | collective-permute-start | bytes 200 | tf_op jit(solution)/shard_map/ppermute | solution.py:23
  159.2 38.0 %collective-permute-start.8 = (bf16[256,1024]{1,0:T(8,128)(2,1)S(1)}, bf16[256,1024]{1,0:T(8,128)(2,1)S(1)}, u32[]{:S(2)}, u32[]{:S(2)}) collective-permute-start(bf16[256,1024]{1,0:T(8,128)(2,1)S(1)} %dynamic-slice_convert_fusion.1), channel_id=1, source_target_pairs={{0,1},{1,2},{2,3},{3,0},{4,5},{5,6},{6,7},{7,4},{8,9},{9,10},{10,1... | collective-permute-start | bytes 1572872 | tf_op jit(solution)/shard_map/ppermute | solution.py:19
  161.2 46.2 %collective-permute-start.11 = (bf16[256,1024]{1,0:T(8,128)(2,1)S(1)}, bf16[256,1024]{1,0:T(8,128)(2,1)S(1)}, u32[]{:S(2)}, u32[]{:S(2)}) collective-permute-start(bf16[256,1024]{1,0:T(8,128)(2,1)S(1)} %dynamic-slice_convert_fusion), channel_id=1, source_target_pairs={{0,1},{1,2},{2,3},{3,0},{4,5},{5,6},{6,7},{7,4},{8,9},{9,10},{10,1... | collective-permute-start | bytes 1572872 | tf_op jit(solution)/shard_map/ppermute | solution.py:19
  198.6 21.8 %collective-permute-start.9 = (bf16[256,1024]{1,0:T(8,128)(2,1)S(1)}, bf16[256,1024]{1,0:T(8,128)(2,1)S(1)}, u32[]{:S(2)}, u32[]{:S(2)}) collective-permute-start(bf16[256,1024]{1,0:T(8,128)(2,1)S(1)} %add_convert_fusion.6), channel_id=1, source_target_pairs={{0,1},{1,2},{2,3},{3,0},{4,5},{5,6},{6,7},{7,4},{8,9},{9,10},{10,1... | collective-permute-start | bytes 1572872 | tf_op jit(solution)/shard_map/ppermute | solution.py:19
  207.1 46.8 %collective-permute-start.7 = (bf16[1,256,4096]{2,1,0:T(8,128)(2,1)}, bf16[1,256,4096]{2,1,0:T(8,128)(2,1)S(1)}, u32[]{:S(2)}, u32[]{:S(2)}) collective-permute-start(bf16[1,256,4096]{2,1,0:T(8,128)(2,1)} %constant_dynamic-slice_fusion), channel_id=1, source_target_pairs={{0,8},{4,12},{8,0},{12,4},{1,9},{5,13},{9,1},{13,5},{2,10},{6,14},... | collective-permute-start | bytes 6291464 | tf_op jit(solution)/shard_map/ppermute | solution.py:23
  208.3 17.0 %collective-permute-start.12 = (bf16[256,1024]{1,0:T(8,128)(2,1)}, bf16[256,1024]{1,0:T(8,128)(2,1)}, u32[]{:S(2)}, u32[]{:S(2)}) collective-permute-start(bf16[256,1024]{1,0:T(8,128)(2,1)} %add_convert_fusion.3), channel_id=1, source_target_pairs={{0,1},{1,2},{2,3},{3,0},{4,5},{5,6},{6,7},{7,4},{8,9},{9,10},{10,1... | collective-permute-start | bytes 1572872 | tf_op jit(solution)/shard_map/ppermute | solution.py:19
  221.8 16.6 %collective-permute-start.10 = (bf16[256,1024]{1,0:T(8,128)(2,1)S(1)}, bf16[256,1024]{1,0:T(8,128)(2,1)S(1)}, u32[]{:S(2)}, u32[]{:S(2)}) collective-permute-start(bf16[256,1024]{1,0:T(8,128)(2,1)S(1)} %add_convert_fusion.5), channel_id=1, source_target_pairs={{0,1},{1,2},{2,3},{3,0},{4,5},{5,6},{6,7},{7,4},{8,9},{9,10},{10,1... | collective-permute-start | bytes 1572872 | tf_op jit(solution)/shard_map/ppermute | solution.py:19
  227.3 20.3 %collective-permute-start.13 = (bf16[256,1024]{1,0:T(8,128)(2,1)}, bf16[256,1024]{1,0:T(8,128)(2,1)S(1)}, u32[]{:S(2)}, u32[]{:S(2)}) collective-permute-start(bf16[256,1024]{1,0:T(8,128)(2,1)} %add_convert_fusion.2), channel_id=1, source_target_pairs={{0,1},{1,2},{2,3},{3,0},{4,5},{5,6},{6,7},{7,4},{8,9},{9,10},{10,1... | collective-permute-start | bytes 1572872 | tf_op jit(solution)/shard_map/ppermute | solution.py:19
  (7 other events, 67.4 us)

commit v2 on v1

--- a/solution.py
+++ b/solution.py
@@ -149,19 +149,15 @@
     pieces = 2
     columns = width // pieces
     shares = []
-    operand = unit_rows
     for piece in range(pieces):
         share = lax.dot_general(
-            operand,
+            unit_rows,
             weight_half[piece * columns : (piece + 1) * columns],
             (((1,), (1,)), ((), ())),
             preferred_element_type=jnp.float32,
         )
         shares.append(lax.optimization_barrier(share))
-        if piece == 0:
-            near = after(near, shares[0][:8, :128])
-            left = (keep.astype(jnp.float32) + near.astype(jnp.float32)).astype(jnp.bfloat16)
-            operand = after(unit_rows, left[0, :8, :128])
+    left = (keep.astype(jnp.float32) + near.astype(jnp.float32)).astype(jnp.bfloat16)
     bit = 2
     while bit < n_mp:
         pairs = left.reshape(-1, 2, out_rows, units)

time: 257 us -> 257 us (level)
  no operation moved by 1% of the time
where the time goes in v2:
time: 257 us; the launch traced here: 256 us
  matrix products  63.5 us (25%)
  other arithmetic  44.3 us (17%)
  Pallas kernels  43.6 us (17%)
  waiting for transfers between devices  42.1 us (16%)
  local copies, waits for them, and re-layouts  40.3 us (16%)
  starting transfers between devices  21.4 us (8%)
    pallas_call x4, Pallas kernels, update_part(): pl.pallas_call(lambda *refs: update_kernel(gain, *refs), grid=(steps, m /...  43.6 us
    ppermute x9, waiting for transfers between devices, ring_up(): return lax.ppermute(value, axis, [(i, (i + 1) % n) for i in range(n)])  36.4 us
    dot_general x4, matrix products, shards(): product = jnp.dot(block, weight_half, preferred_element_type=jnp.float32)  34.7 us
    dot_general x2, matrix products, shards(): lax.dot_general(unit_rows, weight_half[piece * columns:(piece + 1) * colu...  23.9 us
    convert_element_type x1, other arithmetic, shards(): weight_half = lax.optimization_barrier(weight.astype(jnp.bfloat16))  17.4 us
    dynamic_update_slice x8, local copies, waits for them, and re-layouts, put(): return lax.dynamic_update_slice(buffer, block, (index * block.shape[0], 0))  15.1 us
    ppermute x13, starting transfers between devices, swap(): return lax.ppermute(value, axis, [(i, i ^ bit) for i in range(n)])  11.5 us
    convert_element_type x1, other arithmetic, shards(): (unit_rows.astype(jnp.float32) * token_factor).astype(jnp.bfloat16)  10.1 us
  transfers between devices with their start and end apart: 22, of which 7 were waited for; matrix products, arithmetic and copies ran while one was open for 56% of the time, Pallas kernels for 17%

profile of v2, /device:TPU:0, one launch (start us, length us, event | category | flops | bytes accessed | tf_op | source)
XLA Modules:
  0.0 256.0 jit_solution(6820774267231647744)
XLA Ops:
  13.6 17.4 %convert_element_type.86 = bf16[2048,4096]{1,0:T(8,128)(2,1)} convert(f32[2048,4096]{1,0:T(8,128)} %param.6) | non-fusion elementwise | flops 8388608 | bytes 50331648 | tf_op jit(solution)/shard_map/convert_element_type | solution.py:101
  30.9 4.3 %broadcast.25.clone = bf16[1024,4096]{1,0:T(8,128)(2,1)} broadcast(bf16[]{:T(256)} %constant.79.clone.1), dimensions={} | broadcast | bytes 8388610 | tf_op jit(solution)/shard_map/broadcast.9
  35.2 11.4 %fusion.8 = bf16[1024,4096]{1,0:T(8,128)(2,1)} fusion(bf16[1024,4096]{1,0:T(8,128)(2,1)} %broadcast.25.clone, s32[]{:T(128)S(6)} %select_n.72, bf16[256,2048]{1,0:T(8,128)(2,1)S(1)} %copy-done.2, bf16[2048,4096]{1,0:T(8,128)(2,1)} %convert_element_type.86), kind=kOutput, calls=%fused_computation.14 | convolution fusion | flops 4296015872 | bytes 19922948 | tf_op jit(solution)/shard_map/dot_general | solution.py:112
  46.7 4.3 %broadcast.25.clone.1 = bf16[1024,4096]{1,0:T(8,128)(2,1)} broadcast(bf16[]{:T(256)} %constant.79.clone.1), dimensions={} | broadcast | bytes 8388610 | tf_op jit(solution)/shard_map/broadcast.9
  58.5 3.1 %collective-permute-start.17 = (f32[4,64,64]{2,1,0:T(8,128)S(1)}, f32[4,64,64]{2,1,0:T(8,128)S(1)}, u32[]{:S(2)}, u32[]{:S(2)}) collective-permute-start(f32[4,64,64]{2,1,0:T(8,128)S(1)} %add.198), channel_id=1, source_target_pairs={{0,2},{1,3},{2,0},{3,1},{4,6},{5,7},{6,4},{7,5},{8,10},{9,11},{10,... | collective-permute-start | bytes 196616 | tf_op jit(solution)/shard_map/ppermute | solution.py:23
  63.0 11.8 %fusion.7 = bf16[1024,4096]{1,0:T(8,128)(2,1)} fusion(bf16[1024,4096]{1,0:T(8,128)(2,1)} %fusion.8, s32[]{:T(128)S(6)} %select_n.73, bf16[256,2048]{0,1:T(8,128)(2,1)S(1)} %collective-permute-done, bf16[2048,4096]{1,0:T(8,128)(2,1)} %convert_element_type.86), kind=kOutput, calls=%fused_computation.12 | convolution fusion | flops 4296015872 | bytes 19922948 | tf_op jit(solution)/shard_map/dot_general | solution.py:112
  75.8 13.3 %collective-permute-done.1 = bf16[256,2048]{0,1:T(8,128)(2,1)S(1)} collective-permute-done((bf16[256,2048]{0,1:T(8,128)(2,1)S(1)}, bf16[256,2048]{0,1:T(8,128)(2,1)S(1)}, u32[]{:S(2)}, u32[]{:S(2)}) %collective-permute-start.1) | collective-permute-done | bytes 1048608 | tf_op jit(solution)/shard_map/ppermute | solution.py:19
  91.9 3.3 %constant_dynamic-update-slice_fusion.6 = bf16[1024,4096]{1,0:T(8,128)(2,1)} fusion(bf16[1024,4096]{1,0:T(8,128)(2,1)} %constant_dynamic-update-slice_fusion.7, bf16[256,4096]{1,0:T(8,128)(2,1)} %collective-permute-done.5, s32[]{:T(128)S(6)} %select_n.82), kind=kLoop, calls=%fused_computation.34 | loop fusion | bytes 4194308 | tf_op jit(solution)/shard_map/dynamic_update_slice | solution.py:35
  95.2 3.2 %constant_dynamic-update-slice_fusion.5 = bf16[1024,4096]{1,0:T(8,128)(2,1)} fusion(bf16[1024,4096]{1,0:T(8,128)(2,1)} %constant_dynamic-update-slice_fusion.6, bf16[256,4096]{1,0:T(8,128)(2,1)} %collective-permute-done.6, s32[]{:T(128)S(6)} %select_n.83), kind=kLoop, calls=%fused_computation.33 | loop fusion | bytes 4194308 | tf_op jit(solution)/shard_map/dynamic_update_slice | solution.py:35
  98.4 5.7 %fusion.6 = bf16[1024,4096]{1,0:T(8,128)(2,1)} fusion(bf16[1024,4096]{1,0:T(8,128)(2,1)} %fusion.7, s32[]{:T(128)S(6)} %select_n.74, bf16[256,2048]{0,1:T(8,128)(2,1)S(1)} %collective-permute-done.1, bf16[2048,4096]{1,0:T(8,128)(2,1)S(1)} %bitcast.28), kind=kOutput, calls=%fused_computation.10 | convolution fusion | flops 4296015872 | bytes 19922948 | tf_op jit(solution)/shard_map/dot_general | solution.py:112
  104.1 13.2 %collective-permute-done.2 = bf16[256,2048]{0,1:T(8,128)(2,1)S(1)} collective-permute-done((bf16[256,2048]{0,1:T(8,128)(2,1)S(1)}, bf16[256,2048]{0,1:T(8,128)(2,1)S(1)}, u32[]{:S(2)}, u32[]{:S(2)}) %collective-permute-start.2) | collective-permute-done | bytes 1048608 | tf_op jit(solution)/shard_map/ppermute | solution.py:19
  119.5 5.8 %fusion.5 = bf16[1024,4096]{1,0:T(8,128)(2,1)} fusion(bf16[1024,4096]{1,0:T(8,128)(2,1)} %fusion.6, s32[]{:T(128)S(6)} %select_n.75, bf16[256,2048]{0,1:T(8,128)(2,1)S(1)} %collective-permute-done.2, bf16[2048,4096]{1,0:T(8,128)(2,1)S(1)} %bitcast.28), kind=kOutput, calls=%fused_computation.8 | convolution fusion | flops 4296015872 | bytes 19922948 | tf_op jit(solution)/shard_map/dot_general | solution.py:112
  125.2 4.7 %dynamic-slice_bitcast_fusion = bf16[2,256,4096]{2,1,0:T(8,128)(2,1)} fusion(bf16[2,2,256,4096]{3,2,1,0:T(8,128)(2,1)} %bitcast, s32[]{:T(128)S(6)} %select_n.77), kind=kLoop, calls=%fused_computation.16 | loop fusion | bytes 8388612 | tf_op jit(solution)/shard_map/jit(dynamic_index_in_dim)/squeeze | solution.py:146
  132.5 12.6 %fusion.2 = f32[1024,1024]{1,0:T(8,128)} fusion(bf16[1024,4096]{1,0:T(8,128)(2,1)} %constant_dynamic-update-slice_fusion.4, bf16[2048,4096]{1,0:T(8,128)(2,1)S(1)} %bitcast.28), kind=kOutput, calls=%fused_computation.3 | convolution fusion | flops 8589934592 | bytes 20971520 | tf_op jit(solution)/shard_map/dot_general | solution.py:153
  145.1 11.2 %fusion = f32[1024,1024]{1,0:T(8,128)S(1)} fusion(bf16[1024,4096]{1,0:T(8,128)(2,1)} %constant_dynamic-update-slice_fusion.4, bf16[2048,4096]{1,0:T(8,128)(2,1)S(1)} %bitcast.28), kind=kOutput, calls=%fused_computation.1 | convolution fusion | flops 8589934592 | bytes 20971520 | tf_op jit(solution)/shard_map/dot_general | solution.py:153
  161.8 10.1 %multiply_convert_fusion.refs_1_ = bf16[1024,4096]{1,0:T(8,128)(2,1)} fusion(bf16[1024,4096]{1,0:T(8,128)(2,1)} %constant_dynamic-update-slice_fusion.4, f32[1024]{0:T(1024)S(1)} %mul.71), kind=kLoop, calls=%fused_computation | loop fusion | flops 12582912 | bytes 16781312 | tf_op jit(solution)/shard_map/convert_element_type | solution.py:196
  172.0 3.4 %copy-done = bf16[1024,4096]{1,0:T(8,128)(2,1)S(1)} copy-done((bf16[1024,4096]{1,0:T(8,128)(2,1)S(1)}, bf16[1024,4096]{1,0:T(8,128)(2,1)}, u32[]{:S(2)}) %copy-start) | copy-done | bytes 8388632
  175.4 10.9 %shard_map.67.refs_3_ = f32[2048,4096]{1,0:T(8,128)} custom-call(bf16[2048,1024]{1,0:T(8,128)(2,1)} %bitcast.4.refs_0_, bf16[1024,4096]{1,0:T(8,128)(2,1)S(1)} %copy-done, bf16[2,2048,4096]{2,1,0:T(8,128)(2,1)} %refs_2_.7), custom_call_target="tpu_custom_call" | custom-call | flops 4294967296 | bytes 25165824 | tf_op jit(solution)/shard_map/pallas_call | solution.py:68
  186.2 10.9 %shard_map.68.refs_3_ = f32[2048,4096]{1,0:T(8,128)} custom-call(bf16[2048,1024]{1,0:T(8,128)(2,1)} %bitcast.4.refs_0_, bf16[1024,4096]{1,0:T(8,128)(2,1)S(1)} %copy-done, bf16[2,2048,4096]{2,1,0:T(8,128)(2,1)} %refs_2_.7, f32[2048,4096]{1,0:T(8,128)} %shard_map.67.refs_3_), custom_call_target="tpu_custom_call", output_to_operand_aliasing={{}: (3, {})} | custom-call | flops 4294967296 | bytes 25165824 | tf_op jit(solution)/shard_map/pallas_call | solution.py:68
  200.6 5.0 %fusion.4 = bf16[2,256,4096]{2,1,0:T(8,128)(2,1)S(1)} fusion(bf16[2,256,4096]{2,1,0:T(8,128)(2,1)} %collective-permute-done.3, bf16[2,2,256,4096]{3,2,1,0:T(8,128)(2,1)} %bitcast, s32[]{:T(128)S(6)} %select_n.76), kind=kLoop, calls=%fused_computation.6 | loop fusion | flops 8388608 | bytes 12582916 | tf_op jit(solution)/shard_map/convert_element_type | solution.py:160
  209.5 10.9 %shard_map.69.refs_3_ = f32[2048,4096]{1,0:T(8,128)} custom-call(bf16[2048,1024]{1,0:T(8,128)(2,1)} %bitcast.4.refs_0_, bf16[1024,4096]{1,0:T(8,128)(2,1)S(1)} %copy-done, bf16[2,2048,4096]{2,1,0:T(8,128)(2,1)} %refs_2_.7, f32[2048,4096]{1,0:T(8,128)} %shard_map.68.refs_3_), custom_call_target="tpu_custom_call", output_to_operand_aliasing={{}: (3, {})} | custom-call | flops 4294967296 | bytes 25165824 | tf_op jit(solution)/shard_map/pallas_call | solution.py:68
  227.4 10.9 %shard_map.70 = f32[2048,4096]{1,0:T(8,128)} custom-call(bf16[2048,1024]{1,0:T(8,128)(2,1)} %bitcast.4.refs_0_, bf16[1024,4096]{1,0:T(8,128)(2,1)S(1)} %copy-done, bf16[2,2048,4096]{2,1,0:T(8,128)(2,1)} %refs_2_.7, f32[2048,4096]{1,0:T(8,128)} %shard_map.69.refs_3_), custom_call_target="tpu_custom_call", output_to_operand_aliasing={{}: (3, {})} | custom-call | flops 4294967296 | bytes 25165824 | tf_op jit(solution)/shard_map/pallas_call | solution.py:68
  239.8 7.8 %collective-permute-done.13 = bf16[256,1024]{1,0:T(8,128)(2,1)S(1)} collective-permute-done((bf16[256,1024]{1,0:T(8,128)(2,1)}, bf16[256,1024]{1,0:T(8,128)(2,1)S(1)}, u32[]{:S(2)}, u32[]{:S(2)}) %collective-permute-start.13) | collective-permute-done | bytes 524320 | tf_op jit(solution)/shard_map/ppermute | solution.py:19
  248.8 5.1 %collective-permute-done.4 = bf16[1,256,4096]{2,1,0:T(8,128)(2,1)S(1)} collective-permute-done((bf16[1,256,4096]{2,1,0:T(8,128)(2,1)}, bf16[1,256,4096]{2,1,0:T(8,128)(2,1)S(1)}, u32[]{:S(2)}, u32[]{:S(2)}) %collective-permute-start.4) | collective-permute-done | bytes 2097184 | tf_op jit(solution)/shard_map/ppermute | solution.py:23
  (89 shorter events, 55.0 us)
Async XLA Ops:
  0.6 90.0 %collective-permute-start.5 = (bf16[256,4096]{1,0:T(8,128)(2,1)}, bf16[256,4096]{1,0:T(8,128)(2,1)}, u32[]{:S(2)}, u32[]{:S(2)}) collective-permute-start(bf16[256,4096]{1,0:T(8,128)(2,1)} %param.5), channel_id=1, source_target_pairs={{0,8},{4,12},{8,0},{12,4},{1,9},{5,13},{9,1},{13,5},{2,10},{6,14},... | collective-permute-start | bytes 6291464 | tf_op jit(solution)/shard_map/ppermute | solution.py:23
  3.7 91.5 %collective-permute-start.6 = (bf16[256,4096]{1,0:T(8,128)(2,1)}, bf16[256,4096]{1,0:T(8,128)(2,1)}, u32[]{:S(2)}, u32[]{:S(2)}) collective-permute-start(bf16[256,4096]{1,0:T(8,128)(2,1)} %param.5), channel_id=1, source_target_pairs={{0,4},{4,0},{8,12},{12,8},{1,5},{5,1},{9,13},{13,9},{2,6},{6,2},{1... | collective-permute-start | bytes 6291464 | tf_op jit(solution)/shard_map/ppermute | solution.py:23
  5.7 52.6 %collective-permute-start.14 = (f32[4,64,64]{2,1,0:T(8,128)S(1)}, f32[4,64,64]{2,1,0:T(8,128)S(1)}, u32[]{:S(2)}, u32[]{:S(2)}) collective-permute-start(f32[4,64,64]{2,1,0:T(8,128)S(1)} %fusion.11), channel_id=1, source_target_pairs={{0,4},{4,0},{8,12},{12,8},{1,5},{5,1},{9,13},{13,9},{2,6},{6,2},{1... | collective-permute-start | bytes 196616 | tf_op jit(solution)/shard_map/ppermute | solution.py:23
  9.2 48.2 %collective-permute-start.16 = (f32[4,64,64]{2,1,0:T(8,128)S(1)}, f32[4,64,64]{2,1,0:T(8,128)}, u32[]{:S(2)}, u32[]{:S(2)}) collective-permute-start(f32[4,64,64]{2,1,0:T(8,128)S(1)} %fusion.12), channel_id=1, source_target_pairs={{0,1},{1,0},{2,3},{3,2},{4,5},{5,4},{6,7},{7,6},{8,9},{9,8},{10,11... | collective-permute-start | bytes 196616 | tf_op jit(solution)/shard_map/ppermute | solution.py:23
  13.1 44.3 %collective-permute-start = (bf16[256,2048]{0,1:T(8,128)(2,1)}, bf16[256,2048]{0,1:T(8,128)(2,1)S(1)}, u32[]{:S(2)}, u32[]{:S(2)}) collective-permute-start(bf16[256,2048]{0,1:T(8,128)(2,1)} %copy.10), channel_id=1, source_target_pairs={{0,1},{1,2},{2,3},{3,0},{4,5},{5,6},{6,7},{7,4},{8,9},{9,10},{10,1... | collective-permute-start | bytes 3145736 | tf_op jit(solution)/shard_map/ppermute | solution.py:19
  58.4 31.4 %collective-permute-start.15 = (f32[4,64,64]{2,1,0:T(8,128)S(1)}, f32[4,64,64]{2,1,0:T(8,128)S(1)}, u32[]{:S(2)}, u32[]{:S(2)}) collective-permute-start(f32[4,64,64]{2,1,0:T(8,128)S(1)} %add.196), channel_id=1, source_target_pairs={{0,8},{4,12},{8,0},{12,4},{1,9},{5,13},{9,1},{13,5},{2,10},{6,14},... | collective-permute-start | bytes 196616 | tf_op jit(solution)/shard_map/ppermute | solution.py:23
  58.5 31.3 %collective-permute-start.17 = (f32[4,64,64]{2,1,0:T(8,128)S(1)}, f32[4,64,64]{2,1,0:T(8,128)S(1)}, u32[]{:S(2)}, u32[]{:S(2)}) collective-permute-start(f32[4,64,64]{2,1,0:T(8,128)S(1)} %add.198), channel_id=1, source_target_pairs={{0,2},{1,3},{2,0},{3,1},{4,6},{5,7},{6,4},{7,5},{8,10},{9,11},{10,... | collective-permute-start | bytes 196616 | tf_op jit(solution)/shard_map/ppermute | solution.py:23
  61.5 27.6 %collective-permute-start.1 = (bf16[256,2048]{0,1:T(8,128)(2,1)S(1)}, bf16[256,2048]{0,1:T(8,128)(2,1)S(1)}, u32[]{:S(2)}, u32[]{:S(2)}) collective-permute-start(bf16[256,2048]{0,1:T(8,128)(2,1)S(1)} %collective-permute-done), channel_id=1, source_target_pairs={{0,1},{1,2},{2,3},{3,0},{4,5},{5,6},{6,7},{7,4},{8,9},{9,10},{10,1... | collective-permute-start | bytes 3145736 | tf_op jit(solution)/shard_map/ppermute | solution.py:19
  63.0 35.4 %slice-start.1 = ((s8[16777216]{0:T(1024)(128)(4,1)}), s8[4194304]{0:T(1024)(128)(4,1)S(1)}, s32[]{:S(2)}) async-start(s8[16777216]{0:T(1024)(128)(4,1)} %bitcast.27), calls=%async_computation.1 | async-start | bytes 8388608
  63.0 35.4 %slice-start.2 = ((s8[16777216]{0:T(1024)(128)(4,1)}), s8[4194304]{0:T(1024)(128)(4,1)S(1)}, s32[]{:S(2)}) async-start(s8[16777216]{0:T(1024)(128)(4,1)} %bitcast.27), calls=%async_computation.2 | async-start | bytes 8388608
  90.0 27.4 %collective-permute-start.18 = (f32[16]{0:T(128)S(1)}, f32[16]{0:T(128)S(1)}, u32[]{:S(2)}, u32[]{:S(2)}) collective-permute-start(f32[16]{0:T(128)S(1)} %fusion.10), channel_id=1, source_target_pairs={{0,4},{4,0},{8,12},{12,8},{1,5},{5,1},{9,13},{13,9},{2,6},{6,2},{1... | collective-permute-start | bytes 200 | tf_op jit(solution)/shard_map/ppermute | solution.py:23
  90.0 27.4 %collective-permute-start.2 = (bf16[256,2048]{0,1:T(8,128)(2,1)S(1)}, bf16[256,2048]{0,1:T(8,128)(2,1)S(1)}, u32[]{:S(2)}, u32[]{:S(2)}) collective-permute-start(bf16[256,2048]{0,1:T(8,128)(2,1)S(1)} %collective-permute-done.1), channel_id=1, source_target_pairs={{0,1},{1,2},{2,3},{3,0},{4,5},{5,6},{6,7},{7,4},{8,9},{9,10},{10,1... | collective-permute-start | bytes 3145736 | tf_op jit(solution)/shard_map/ppermute | solution.py:19
  90.7 40.4 %collective-permute-start.7 = (bf16[256,4096]{1,0:T(8,128)(2,1)}, bf16[256,4096]{1,0:T(8,128)(2,1)S(1)}, u32[]{:S(2)}, u32[]{:S(2)}) collective-permute-start(bf16[256,4096]{1,0:T(8,128)(2,1)} %collective-permute-done.5), channel_id=1, source_target_pairs={{0,4},{4,0},{8,12},{12,8},{1,5},{5,1},{9,13},{13,9},{2,6},{6,2},{1... | collective-permute-start | bytes 6291464 | tf_op jit(solution)/shard_map/ppermute | solution.py:23
  117.6 13.5 %collective-permute-start.19 = (f32[16]{0:T(128)S(1)}, f32[16]{0:T(128)S(1)}, u32[]{:S(2)}, u32[]{:S(2)}) collective-permute-start(f32[16]{0:T(128)S(1)} %add_dynamic-update-slice_fusion), channel_id=1, source_target_pairs={{0,8},{4,12},{8,0},{12,4},{1,9},{5,13},{9,1},{13,5},{2,10},{6,14},... | collective-permute-start | bytes 200 | tf_op jit(solution)/shard_map/ppermute | solution.py:23
  129.9 70.7 %collective-permute-start.3 = (bf16[2,256,4096]{2,1,0:T(8,128)(2,1)}, bf16[2,256,4096]{2,1,0:T(8,128)(2,1)}, u32[]{:S(2)}, u32[]{:S(2)}) collective-permute-start(bf16[2,256,4096]{2,1,0:T(8,128)(2,1)} %dynamic-slice_bitcast_fusion), channel_id=1, source_target_pairs={{0,4},{4,0},{8,12},{12,8},{1,5},{5,1},{9,13},{13,9},{2,6},{6,2},{1... | collective-permute-start | bytes 12582920 | tf_op jit(solution)/shard_map/ppermute | solution.py:23
  131.1 25.4 %collective-permute-start.20 = (f32[16]{0:T(128)S(1)}, f32[16]{0:T(128)S(1)}, u32[]{:S(2)}, u32[]{:S(2)}) collective-permute-start(f32[16]{0:T(128)S(1)} %add.202), channel_id=1, source_target_pairs={{0,1},{1,0},{2,3},{3,2},{4,5},{5,4},{6,7},{7,6},{8,9},{9,8},{10,11... | collective-permute-start | bytes 200 | tf_op jit(solution)/shard_map/ppermute | solution.py:23
  156.4 5.3 %collective-permute-start.21 = (f32[16]{0:T(128)S(1)}, f32[16]{0:T(128)S(1)}, u32[]{:S(2)}, u32[]{:S(2)}) collective-permute-start(f32[16]{0:T(128)S(1)} %add.203), channel_id=1, source_target_pairs={{0,2},{1,3},{2,0},{3,1},{4,6},{5,7},{6,4},{7,5},{8,10},{9,11},{10,... | collective-permute-start | bytes 200 | tf_op jit(solution)/shard_map/ppermute | solution.py:23
  159.2 38.0 %collective-permute-start.8 = (bf16[256,1024]{1,0:T(8,128)(2,1)S(1)}, bf16[256,1024]{1,0:T(8,128)(2,1)S(1)}, u32[]{:S(2)}, u32[]{:S(2)}) collective-permute-start(bf16[256,1024]{1,0:T(8,128)(2,1)S(1)} %dynamic-slice_convert_fusion.1), channel_id=1, source_target_pairs={{0,1},{1,2},{2,3},{3,0},{4,5},{5,6},{6,7},{7,4},{8,9},{9,10},{10,1... | collective-permute-start | bytes 1572872 | tf_op jit(solution)/shard_map/ppermute | solution.py:19
  161.2 46.2 %collective-permute-start.11 = (bf16[256,1024]{1,0:T(8,128)(2,1)S(1)}, bf16[256,1024]{1,0:T(8,128)(2,1)S(1)}, u32[]{:S(2)}, u32[]{:S(2)}) collective-permute-start(bf16[256,1024]{1,0:T(8,128)(2,1)S(1)} %dynamic-slice_convert_fusion), channel_id=1, source_target_pairs={{0,1},{1,2},{2,3},{3,0},{4,5},{5,6},{6,7},{7,4},{8,9},{9,10},{10,1... | collective-permute-start | bytes 1572872 | tf_op jit(solution)/shard_map/ppermute | solution.py:19
  198.6 21.8 %collective-permute-start.9 = (bf16[256,1024]{1,0:T(8,128)(2,1)S(1)}, bf16[256,1024]{1,0:T(8,128)(2,1)S(1)}, u32[]{:S(2)}, u32[]{:S(2)}) collective-permute-start(bf16[256,1024]{1,0:T(8,128)(2,1)S(1)} %add_convert_fusion.6), channel_id=1, source_target_pairs={{0,1},{1,2},{2,3},{3,0},{4,5},{5,6},{6,7},{7,4},{8,9},{9,10},{10,1... | collective-permute-start | bytes 1572872 | tf_op jit(solution)/shard_map/ppermute | solution.py:19
  207.1 46.8 %collective-permute-start.4 = (bf16[1,256,4096]{2,1,0:T(8,128)(2,1)}, bf16[1,256,4096]{2,1,0:T(8,128)(2,1)S(1)}, u32[]{:S(2)}, u32[]{:S(2)}) collective-permute-start(bf16[1,256,4096]{2,1,0:T(8,128)(2,1)} %constant_dynamic-slice_fusion), channel_id=1, source_target_pairs={{0,8},{4,12},{8,0},{12,4},{1,9},{5,13},{9,1},{13,5},{2,10},{6,14},... | collective-permute-start | bytes 6291464 | tf_op jit(solution)/shard_map/ppermute | solution.py:23
  208.3 17.0 %collective-permute-start.12 = (bf16[256,1024]{1,0:T(8,128)(2,1)}, bf16[256,1024]{1,0:T(8,128)(2,1)}, u32[]{:S(2)}, u32[]{:S(2)}) collective-permute-start(bf16[256,1024]{1,0:T(8,128)(2,1)} %add_convert_fusion.3), channel_id=1, source_target_pairs={{0,1},{1,2},{2,3},{3,0},{4,5},{5,6},{6,7},{7,4},{8,9},{9,10},{10,1... | collective-permute-start | bytes 1572872 | tf_op jit(solution)/shard_map/ppermute | solution.py:19
  221.8 16.6 %collective-permute-start.10 = (bf16[256,1024]{1,0:T(8,128)(2,1)S(1)}, bf16[256,1024]{1,0:T(8,128)(2,1)S(1)}, u32[]{:S(2)}, u32[]{:S(2)}) collective-permute-start(bf16[256,1024]{1,0:T(8,128)(2,1)S(1)} %add_convert_fusion.5), channel_id=1, source_target_pairs={{0,1},{1,2},{2,3},{3,0},{4,5},{5,6},{6,7},{7,4},{8,9},{9,10},{10,1... | collective-permute-start | bytes 1572872 | tf_op jit(solution)/shard_map/ppermute | solution.py:19
  227.3 20.3 %collective-permute-start.13 = (bf16[256,1024]{1,0:T(8,128)(2,1)}, bf16[256,1024]{1,0:T(8,128)(2,1)S(1)}, u32[]{:S(2)}, u32[]{:S(2)}) collective-permute-start(bf16[256,1024]{1,0:T(8,128)(2,1)} %add_convert_fusion.2), channel_id=1, source_target_pairs={{0,1},{1,2},{2,3},{3,0},{4,5},{5,6},{6,7},{7,4},{8,9},{9,10},{10,1... | collective-permute-start | bytes 1572872 | tf_op jit(solution)/shard_map/ppermute | solution.py:19
  (7 other events, 67.4 us)
